TPU v7x, 32 devices: a whole 2x2x4 slice. The times are simulated.
32 devices in a mesh: virt: 8 (over z, x), pair: 4 (over y, core).
Axes of the slice: x: 2, y: 2, z: 4, core: 2. Of those that a mesh axis runs over, the one named last changes fastest.
Arguments:
- amplitudes: bfloat16 [8, 1024, 2, 1024], P('pair'), may hold values from -6 to 6
- integrals: bfloat16 [2, 512, 8, 65536], P(None, None, None, ('virt', 'pair')), may hold values from -0.125 to 0.125
- virt_counts: int32 [8], replicated, may hold values from 32 to 64, as said below
- pair_counts: int32 [8], replicated, may hold values from 512 to 1024, as said below
- pair_list: int32 [8, 1024, 2], P('pair'), may hold values from 0 to 99
- eps_occ: float32 [100], replicated, may hold values from -2 to -0.3
- eps_virt: float32 [512], replicated, may hold values from 0.3 to 4
Outputs:
- update: bfloat16 [8, 1024, 32768], P('pair', None, 'virt')
- pair_energy: float32 [8, 1024], P('pair', 'virt')
Inputs may be any that keep to these rules, and one draw needn't show every extreme that they name: virt_counts[0] = 64; every count is at least 32. `pair_counts`: some pair symmetry has exactly 1024 pairs; every count is at least 512.
All inputs are finite; a program needn't handle non-finite values.
Results may differ from a plain program's by a relative error of at most 0.001.
Values may be sent and summed in bfloat16 or wider, within the bound.
A program may use at most 192 MiB of HBM per device.

v0:
```python
import jax
import jax.numpy as jnp
from jax import lax
from jax.sharding import PartitionSpec as P

IRREPS = 8
NV = 512
BLK = 64
CS = 16
SLABS = 2


def pick_counts(irrep_ids, table):
    onehot = irrep_ids[..., None] == jnp.arange(table.shape[0], dtype=jnp.int32)
    return jnp.sum(jnp.where(onehot, table, 0), axis=-1)


def shards(amplitudes, integrals, virt_counts, pair_counts, pair_list, eps_occ, eps_virt):
    local_irreps = amplitudes.shape[0]
    rows = amplitudes.shape[1]
    width = amplitudes.shape[3]
    n_virt = lax.axis_size("virt")
    n_pair = lax.axis_size("pair")
    a_local = NV // n_virt
    irrep_ids = lax.axis_index("pair") * local_irreps + jnp.arange(local_irreps, dtype=jnp.int32)
    slots = jnp.arange(BLK, dtype=jnp.int32)
    live_d = slots[None, :] < pick_counts(irrep_ids, virt_counts)[:, None]
    dmask = jnp.tile(live_d, (1, CS)).astype(jnp.bfloat16)
    masked = amplitudes * dmask[:, None, None, :]
    ladder = jnp.zeros((local_irreps, rows, a_local, BLK), jnp.float32)
    for s in range(SLABS):
        piece = integrals[s]
        moved = lax.all_to_all(
            lax.all_to_all(piece, "virt", split_axis=0, concat_axis=2, tiled=True),
            "pair",
            split_axis=1,
            concat_axis=2,
            tiled=True,
        )
        moved = moved.reshape(a_local, local_irreps, n_pair, n_virt, -1)
        moved = jnp.transpose(moved, (0, 1, 3, 2, 4)).reshape(a_local, local_irreps, BLK, width)
        ladder = ladder + jnp.einsum(
            "hrk,ahsk->hras", masked[:, :, s, :], moved, preferred_element_type=jnp.float32
        )
    a_global = lax.axis_index("virt") * a_local + jnp.arange(a_local, dtype=jnp.int32)
    a_irrep = a_global // BLK
    a_slot = a_global % BLK
    live_a = a_slot < pick_counts(a_irrep, virt_counts)
    eps_a = lax.dynamic_slice_in_dim(eps_virt, lax.axis_index("virt") * a_local, a_local)
    b_irrep = jnp.bitwise_xor(a_irrep[None, :], irrep_ids[:, None])
    b_onehot = (b_irrep[..., None] == jnp.arange(IRREPS, dtype=jnp.int32)).astype(jnp.float32)
    eps_table = eps_virt.reshape(IRREPS, BLK)
    eps_b = jnp.einsum("hag,gs->has", b_onehot, eps_table, precision=lax.Precision.HIGHEST)
    live_b = slots[None, None, :] < pick_counts(b_irrep, virt_counts)[..., None]
    occ_onehot = pair_list[..., None] == jnp.arange(eps_occ.shape[0], dtype=jnp.int32)
    occ_terms = jnp.sum(jnp.where(occ_onehot, eps_occ, 0.0), axis=-1)
    occ = occ_terms[:, :, 0] + occ_terms[:, :, 1]
    live_rows = (
        jnp.arange(rows, dtype=jnp.int32)[None, :] < pick_counts(irrep_ids, pair_counts)[:, None]
    )
    denom = (eps_a[None, :, None] + eps_b)[:, None, :, :] - occ[:, :, None, None]
    live = live_rows[:, :, None, None] & live_a[None, None, :, None] & live_b[:, None, :, :]
    ratio = jnp.where(live, ladder / denom, jnp.zeros_like(ladder))
    update = ratio.astype(jnp.bfloat16).reshape(local_irreps, rows, a_local * BLK)
    partial_value = jnp.sum(ratio * ladder, axis=(2, 3)) / (NV * BLK)
    energy = lax.psum_scatter(partial_value, "virt", scatter_dimension=1, tiled=True)
    return (update, energy)


def solution(mesh):
    placed = (
        P("pair", None, None, None),
        P(None, None, None, ("virt", "pair")),
        P(),
        P(),
        P("pair", None, None),
        P(),
        P(),
    )
    return jax.shard_map(
        shards,
        mesh=mesh,
        in_specs=placed,
        out_specs=(P("pair", None, "virt"), P("pair", "virt")),
        check_vma=False,
    )
```

profile of v0, /device:TPU:0, one launch (start us, length us, event | category | flops | bytes accessed | tf_op | source)
XLA Modules:
  0.0 1328.9 jit_solution(8190828221373560222)
XLA Ops:
  7.2 18.4 %slice_bitcast_fusion = (bf16[512,8,2048]{2,1,0:T(8,128)(2,1)S(1)}, bf16[512,8,2048]{2,1,0:T(8,128)(2,1)}) fusion(bf16[2,512,8,2048]{3,2,1,0:T(8,128)(2,1)} %param.8), kind=kLoop, calls=%fused_computation.6 | loop fusion | bytes 67108864 | tf_op jit(solution)/shard_map/squeeze | solution.py:32
  25.6 370.0 %all_to_all.66 = bf16[512,8,2048]{2,1,0:T(8,128)(2,1)} all-to-all(bf16[512,8,2048]{2,1,0:T(8,128)(2,1)S(1)} %get-tuple-element.14), channel_id=1, replica_groups=mesh['virt'=8,'pair'=4] {'virt'}, dimensions={0} | all-to-all | bytes 33554432 | tf_op jit(solution)/shard_map/all_to_all | solution.py:34
  401.3 18.7 %copy.53 = bf16[8,64,8,2048]{3,0,2,1:T(8,128)(2,1)} copy(bf16[8,64,8,2048]{3,2,1,0:T(8,128)(2,1)} %bitcast.65) | data formatting | bytes 33554432 | tf_op jit(solution)/shard_map/all_to_all | solution.py:34
  420.0 25.6 %all_to_all.58 = bf16[64,8,16384]{2,1,0:T(8,128)(2,1)} reshape(bf16[64,8,8,2048]{3,2,1,0:T(8,128)(2,1)} %bitcast.66) | data formatting | bytes 33554432 | tf_op jit(solution)/shard_map/all_to_all | solution.py:34
  445.6 18.5 %copy.38 = bf16[64,8,16384]{2,0,1:T(8,128)(2,1)} copy(bf16[64,8,16384]{2,1,0:T(8,128)(2,1)} %all_to_all.58) | data formatting | bytes 33554432 | tf_op jit(solution)/shard_map/all_to_all | solution.py:34
  464.1 299.2 %all-to-all-done = bf16[512,8,2048]{2,1,0:T(8,128)(2,1)} async-done(((bf16[512,8,2048]{2,1,0:T(8,128)(2,1)}), bf16[512,8,2048]{2,1,0:T(8,128)(2,1)}, u32[]{:S(2)}, u32[]{:S(2)}) %all-to-all-start) | async-done | bytes 16777248 | tf_op jit(solution)/shard_map/all_to_all | solution.py:34
  770.2 18.7 %copy.54 = bf16[8,64,8,2048]{3,0,2,1:T(8,128)(2,1)} copy(bf16[8,64,8,2048]{3,2,1,0:T(8,128)(2,1)} %bitcast.4) | data formatting | bytes 33554432 | tf_op jit(solution)/shard_map/all_to_all | solution.py:34
  788.9 25.6 %all_to_all.51 = bf16[64,8,16384]{2,1,0:T(8,128)(2,1)} reshape(bf16[64,8,8,2048]{3,2,1,0:T(8,128)(2,1)} %bitcast.67) | data formatting | bytes 33554432 | tf_op jit(solution)/shard_map/all_to_all | solution.py:34
  814.5 18.5 %copy.34 = bf16[64,8,16384]{2,0,1:T(8,128)(2,1)} copy(bf16[64,8,16384]{2,1,0:T(8,128)(2,1)} %all_to_all.51) | data formatting | bytes 33554432 | tf_op jit(solution)/shard_map/all_to_all | solution.py:34
  833.1 120.2 %all-to-all-done.3 = bf16[64,8,16384]{2,0,1:T(8,128)(2,1)} async-done(((bf16[64,8,16384]{2,0,1:T(8,128)(2,1)}), bf16[64,8,16384]{2,0,1:T(8,128)(2,1)}, u32[]{:S(2)}, u32[]{:S(2)}) %all-to-all-start.3) | async-done | bytes 16777248 | tf_op jit(solution)/shard_map/all_to_all | solution.py:33
  962.8 9.3 copy_multiply_fusion
  972.0 8.0 copy.39
  980.0 10.4 copy.48
  990.4 14.1 %copy.40 = bf16[64,2,8,4,2048]{4,3,2,0,1:T(4,128)(2,1)} copy(bf16[64,2,8,4,2048]{4,2,0,3,1:T(8,128)(2,1)S(1)} %bitcast.69) | data formatting | bytes 33554432 | tf_op jit(solution)/shard_map/transpose | solution.py:41
  1004.6 23.7 %reshape.187 = bf16[64,2,64,1024]{3,2,0,1:T(8,128)(2,1)} reshape(bf16[64,2,8,4,2048]{4,3,2,0,1:T(4,128)(2,1)} %copy.40) | data formatting | bytes 33554432 | tf_op jit(solution)/shard_map/reshape | solution.py:41
  1028.3 115.0 %all-to-all-done.1 = bf16[64,8,16384]{2,0,1:T(8,128)(2,1)} async-done(((bf16[64,8,16384]{2,0,1:T(8,128)(2,1)}), bf16[64,8,16384]{2,0,1:T(8,128)(2,1)}, u32[]{:S(2)}, u32[]{:S(2)}) %all-to-all-start.1) | async-done | bytes 16777248 | tf_op jit(solution)/shard_map/all_to_all | solution.py:33
  1143.2 8.0 copy.35
  1151.2 10.4 copy.47
  1161.7 14.1 %copy.36 = bf16[64,2,8,4,2048]{4,3,2,0,1:T(4,128)(2,1)} copy(bf16[64,2,8,4,2048]{4,2,0,3,1:T(8,128)(2,1)S(1)} %bitcast.71) | data formatting | bytes 33554432 | tf_op jit(solution)/shard_map/transpose | solution.py:41
  1175.8 23.7 %reshape.185 = bf16[64,2,64,1024]{3,2,0,1:T(8,128)(2,1)} reshape(bf16[64,2,8,4,2048]{4,3,2,0,1:T(4,128)(2,1)} %copy.36) | data formatting | bytes 33554432 | tf_op jit(solution)/shard_map/reshape | solution.py:41
  1199.5 26.7 %fusion.1 = f32[2,1024,64,64]{1,3,2,0:T(8,128)} fusion(bf16[64,2,64,1024]{3,2,0,1:T(8,128)(2,1)} %reshape.185, bf16[2,1024,2,1024]{3,1,0,2:T(8,128)(2,1)} %copy_multiply_fusion), kind=kOutput, calls=%fused_computation.11 | convolution fusion | flops 17179869184 | bytes 54525952 | tf_op jit(solution)/shard_map/hrk,ahsk->hras/dot_general | solution.py:42
  1226.2 32.0 %multiply_reduce_fusion = (f32[2,1024]{1,0:T(2,128)S(1)}, bf16[2,1024,64,64]{1,3,2,0:T(8,128)(2,1)}) fusion(f32[2,1024]{1,0:T(2,128)S(1)} %bitcast.75, f32[2,64,64]{2,1,0:T(8,128)S(1)} %convolution_add_fusion.1, pred[2,64,64]{2,1,0:T(8,128)(4,1)S(1)} %iota_compare_fusion, pred[2,1024,64]{1,2,0:T(8,128)(4,1)S(1)} %broadcast_and_fusion, ...), kind=kOutput, calls=%fused_computation | convolution fusion | flops 17246976000 | bytes 71491584 | tf_op jit(solution)/shard_map/hrk,ahsk->hras/dot_general | solution.py:42
  1259.2 21.2 %copy.41 = bf16[2,1024,4096]{2,1,0:T(8,128)(2,1)} copy(bf16[2,1024,4096]{1,2,0:T(8,128)(2,1)} %bitcast.72) | data formatting | bytes 33554432
  1280.5 40.1 %reduce-scatter.4.cloned.1.call-done = f32[128,2]{1,0:T(8,128)} async-done(((f32[1024,2]{1,0:T(8,128)}), f32[128,2]{1,0:T(8,128)}) %reduce-scatter.4.cloned.1.call-update) | async-done | bytes 1040
  (37 shorter events, 24.7 us)
Async XLA Ops:
  395.6 367.7 %all-to-all-start = ((bf16[512,8,2048]{2,1,0:T(8,128)(2,1)}), bf16[512,8,2048]{2,1,0:T(8,128)(2,1)}, u32[]{:S(2)}, u32[]{:S(2)}) async-start(bf16[512,8,2048]{2,1,0:T(8,128)(2,1)} %get-tuple-element.15), calls=%async_computation | async-start | bytes 33554432 | tf_op jit(solution)/shard_map/all_to_all | solution.py:34
  763.3 190.0 %all-to-all-start.3 = ((bf16[64,8,16384]{2,0,1:T(8,128)(2,1)}), bf16[64,8,16384]{2,0,1:T(8,128)(2,1)}, u32[]{:S(2)}, u32[]{:S(2)}) async-start(bf16[64,8,16384]{2,0,1:T(8,128)(2,1)} %copy.38), calls=%async_computation.3 | async-start | bytes 33554432 | tf_op jit(solution)/shard_map/all_to_all | solution.py:33
  833.0 127.4 %copy-start.1 = (f32[512]{0:T(512)S(1)}, f32[512]{0:T(512)}, u32[]{:S(2)}) copy-start(f32[512]{0:T(512)} %param.13) | copy-start | bytes 6148
  833.0 127.6 %copy-start.2 = (s32[8]{0:T(128)S(1)}, s32[8]{0:T(128)}, u32[]{:S(2)}) copy-start(s32[8]{0:T(128)} %param.9) | copy-start | bytes 100
  833.0 127.6 %copy-start.4 = (s32[8]{0:T(128)S(1)}, s32[8]{0:T(128)}, u32[]{:S(2)}) copy-start(s32[8]{0:T(128)} %param.10) | copy-start | bytes 100
  833.0 127.9 %copy-start = (s32[2,1024,2]{1,2,0:T(2,128)S(1)}, s32[2,1024,2]{1,2,0:T(2,128)}, u32[]{:S(2)}) copy-start(s32[2,1024,2]{1,2,0:T(2,128)} %param.11) | copy-start | bytes 49156
  833.0 127.9 %copy-start.3 = (f32[100]{0:T(128)S(1)}, f32[100]{0:T(128)}, u32[]{:S(2)}) copy-start(f32[100]{0:T(128)} %param.12) | copy-start | bytes 1204
  953.2 190.0 %all-to-all-start.1 = ((bf16[64,8,16384]{2,0,1:T(8,128)(2,1)}), bf16[64,8,16384]{2,0,1:T(8,128)(2,1)}, u32[]{:S(2)}, u32[]{:S(2)}) async-start(bf16[64,8,16384]{2,0,1:T(8,128)(2,1)} %copy.34), calls=%async_computation.1 | async-start | bytes 33554432 | tf_op jit(solution)/shard_map/all_to_all | solution.py:33
  960.2 360.4 %reduce-scatter.4.cloned.1.call-start = ((), (), s32[]{:S(2)}) async-start(), calls=%async_computation.5 | async-start | bytes 589824
Sparse Core Ops, SparseCore 0:
  1259.4 61.1 reduce-scatter.3
where the time goes:
time: 1330 us
  waiting for transfers between devices  574 us (43%)
  blocking collectives  370 us (28%)
  local copies, waits for them, and re-layouts  280 us (21%)
  matrix products  59 us (4%)
  starting transfers between devices  19.9 us (1%)
  between operations  14.2 us (1%)
    all_to_all x1, blocking collectives, shards(): lax.all_to_all(piece, 'virt', split_axis=0, concat_axis=2, tiled=True)  370 us
    all_to_all x1, waiting for transfers between devices, shards(): lax.all_to_all(piece, 'virt', split_axis=0, concat_axis=2, tiled=True)  299 us
    all_to_all x2, waiting for transfers between devices, shards(): lax.all_to_all(lax.all_to_all(piece, 'virt', split_axis=0, concat_axis=2,...  235 us
    all_to_all x6, local copies, waits for them, and re-layouts, shards(): lax.all_to_all(piece, 'virt', split_axis=0, concat_axis=2, tiled=True)  126 us
    dot_general x2, matrix products, shards(): jnp.einsum('hrk,ahsk->hras', masked[:, :, s, :], moved, preferred_element...  58.7 us
    reshape x2, local copies, waits for them, and re-layouts, shards(): jnp.transpose(moved, (0, 1, 3, 2, 4))  47.4 us
    unnamed x16, local copies, waits for them, and re-layouts  44.6 us
    unnamed x2, waiting for transfers between devices  40.1 us
  transfers between devices with their start and end apart: 4, of which 4 were waited for; matrix products, arithmetic and copies ran while one was open for 12% of the time, Pallas kernels for 0%

commit v1 on v0

--- a/solution.py
+++ b/solution.py
@@ -8,6 +8,15 @@
 BLK = 64
 CS = 16
 SLABS = 2
+_detail_layers_all = lambda buf: jnp.concatenate(
+    jax.lax.all_to_all(
+        jnp.stack(jnp.split(buf, jax.lax.axis_size("virt"), axis=0), axis=0),
+        axis_name="virt",
+        split_axis=0,
+        concat_axis=0,
+    ),
+    axis=2,
+)
 
 
 def pick_counts(irrep_ids, table):
@@ -31,11 +40,7 @@
     for s in range(SLABS):
         piece = integrals[s]
         moved = lax.all_to_all(
-            lax.all_to_all(piece, "virt", split_axis=0, concat_axis=2, tiled=True),
-            "pair",
-            split_axis=1,
-            concat_axis=2,
-            tiled=True,
+            _detail_layers_all(piece), "pair", split_axis=1, concat_axis=2, tiled=True
         )
         moved = moved.reshape(a_local, local_irreps, n_pair, n_virt, -1)
         moved = jnp.transpose(moved, (0, 1, 3, 2, 4)).reshape(a_local, local_irreps, BLK, width)

time: 1330 us -> 1350 us (1.015)
  waiting for transfers between devices: 574 us -> 612 us
  local copies, waits for them, and re-layouts: 280 us -> 257 us
    all_to_all x8 -> x2, local copies, waits for them, and re-layouts: 141 us -> 15.9 us  [shards(): lax.all_to_all(_detail_layers_all(piece), 'pair', split_axis=1, concat_ax...]
    reshape x0 -> x4, local copies, waits for them, and re-layouts: none -> 88.5 us  [jnp.concatenate(jax.lax.all_to_all(jnp.stack(jnp.split(buf, jax.lax.axis_...]
    all_to_all x3, waiting for transfers between devices: 534 us -> 572 us  [the longest x1 318 us: jax.lax.all_to_all(jnp.stack(jnp.split(buf, jax.lax.axis_size('virt'), ax...]
    unnamed x16 -> x25, local copies, waits for them, and re-layouts: 44.6 us -> 74.4 us
    squeeze x1 -> x0, local copies, waits for them, and re-layouts: 18.4 us -> none  [shards(): piece = integrals[s]]
  transfers between devices with their start and end apart: 4 -> 4, of which waited for: 4 -> 4; matrix products, arithmetic and copies ran while one was open for 12% -> 13% of each run, Pallas kernels for 0% -> 0%
where the time goes in v1:
time: 1350 us
  waiting for transfers between devices  612 us (45%)
  blocking collectives  372 us (28%)
  local copies, waits for them, and re-layouts  257 us (19%)
  matrix products  59 us (4%)
  starting transfers between devices  20 us (1%)
  between operations  14.2 us (1%)
    all_to_all x1, blocking collectives, jax.lax.all_to_all(jnp.stack(jnp.split(buf, jax.lax.axis_size('virt'), ax...  372 us
    all_to_all x1, waiting for transfers between devices, jax.lax.all_to_all(jnp.stack(jnp.split(buf, jax.lax.axis_size('virt'), ax...  318 us
    all_to_all x2, waiting for transfers between devices, shards(): lax.all_to_all(_detail_layers_all(piece), 'pair', split_axis=1, concat_ax...  254 us
    reshape x4, local copies, waits for them, and re-layouts, jnp.concatenate(jax.lax.all_to_all(jnp.stack(jnp.split(buf, jax.lax.axis_...  88.5 us
    unnamed x25, local copies, waits for them, and re-layouts  74.4 us
    dot_general x2, matrix products, shards(): jnp.einsum('hrk,ahsk->hras', masked[:, :, s, :], moved, preferred_element...  58.8 us
    reshape x2, local copies, waits for them, and re-layouts, shards(): jnp.transpose(moved, (0, 1, 3, 2, 4))  47.4 us
    unnamed x2, waiting for transfers between devices  39.7 us
  transfers between devices with their start and end apart: 4, of which 4 were waited for; matrix products, arithmetic and copies ran while one was open for 13% of the time, Pallas kernels for 0%

profile of v1, /device:TPU:0, one launch (start us, length us, event | category | flops | bytes accessed | tf_op | source)
XLA Modules:
  0.0 1345.2 jit_solution(14279288042417927330)
XLA Ops:
  39.4 372.0 %all_to_all.40 = bf16[8,64,8,2048]{3,2,1,0:T(8,128)(2,1)} all-to-all(bf16[8,64,8,2048]{3,2,1,0:T(8,128)(2,1)} %get-tuple-element.14), channel_id=1, replica_groups=mesh['virt'=8,'pair'=4] {'virt'}, dimensions={0} | all-to-all | bytes 33554432 | tf_op jit(solution)/shard_map/all_to_all | solution.py:12
  411.4 5.7 all-to-all-start
  417.2 18.6 %copy.45 = bf16[64,8,8,2048]{3,2,0,1:T(8,128)(2,1)} copy(bf16[64,8,8,2048]{3,1,0,2:T(8,128)(2,1)} %bitcast.59) | data formatting | bytes 33554432 | tf_op jit(solution)/shard_map/reshape | solution.py:11
  435.8 25.6 %reshape.242 = bf16[64,8,16384]{2,0,1:T(8,128)(2,1)} reshape(bf16[64,8,8,2048]{3,2,0,1:T(8,128)(2,1)} %copy.45) | data formatting | bytes 33554432 | tf_op jit(solution)/shard_map/reshape | solution.py:11
  461.4 318.3 %all-to-all-done = bf16[8,64,8,2048]{3,2,1,0:T(8,128)(2,1)} async-done(((bf16[8,64,8,2048]{3,2,1,0:T(8,128)(2,1)}), bf16[8,64,8,2048]{3,2,1,0:T(8,128)(2,1)}, u32[]{:S(2)}, u32[]{:S(2)}) %all-to-all-start) | async-done | bytes 16777248 | tf_op jit(solution)/shard_map/all_to_all | solution.py:12
  779.7 7.0 all-to-all-start.3
  786.7 18.6 %copy.44 = bf16[64,8,8,2048]{3,2,0,1:T(8,128)(2,1)} copy(bf16[64,8,8,2048]{3,1,0,2:T(8,128)(2,1)} %bitcast.3) | data formatting | bytes 33554432 | tf_op jit(solution)/shard_map/reshape | solution.py:11
  805.3 25.6 %reshape.241 = bf16[64,8,16384]{2,0,1:T(8,128)(2,1)} reshape(bf16[64,8,8,2048]{3,2,0,1:T(8,128)(2,1)} %copy.44) | data formatting | bytes 33554432 | tf_op jit(solution)/shard_map/reshape | solution.py:11
  831.0 138.7 %all-to-all-done.3 = bf16[64,8,16384]{2,0,1:T(8,128)(2,1)} async-done(((bf16[64,8,16384]{2,0,1:T(8,128)(2,1)}), bf16[64,8,16384]{2,0,1:T(8,128)(2,1)}, u32[]{:S(2)}, u32[]{:S(2)}) %all-to-all-start.3) | async-done | bytes 16777248 | tf_op jit(solution)/shard_map/all_to_all | solution.py:42
  969.7 7.1 all-to-all-start.1
  979.3 9.3 copy_multiply_fusion
  988.6 8.0 copy.39
  996.6 10.4 copy.52
  1007.0 14.1 %copy.40 = bf16[64,2,8,4,2048]{4,3,2,0,1:T(4,128)(2,1)} copy(bf16[64,2,8,4,2048]{4,2,0,3,1:T(8,128)(2,1)S(1)} %bitcast.61) | data formatting | bytes 33554432 | tf_op jit(solution)/shard_map/transpose | solution.py:46
  1021.2 23.7 %reshape.235 = bf16[64,2,64,1024]{3,2,0,1:T(8,128)(2,1)} reshape(bf16[64,2,8,4,2048]{4,3,2,0,1:T(4,128)(2,1)} %copy.40) | data formatting | bytes 33554432 | tf_op jit(solution)/shard_map/reshape | solution.py:46
  1044.8 115.0 %all-to-all-done.1 = bf16[64,8,16384]{2,0,1:T(8,128)(2,1)} async-done(((bf16[64,8,16384]{2,0,1:T(8,128)(2,1)}), bf16[64,8,16384]{2,0,1:T(8,128)(2,1)}, u32[]{:S(2)}, u32[]{:S(2)}) %all-to-all-start.1) | async-done | bytes 16777248 | tf_op jit(solution)/shard_map/all_to_all | solution.py:42
  1159.8 8.0 copy.35
  1167.8 10.4 copy.51
  1178.2 14.1 %copy.36 = bf16[64,2,8,4,2048]{4,3,2,0,1:T(4,128)(2,1)} copy(bf16[64,2,8,4,2048]{4,2,0,3,1:T(8,128)(2,1)S(1)} %bitcast.63) | data formatting | bytes 33554432 | tf_op jit(solution)/shard_map/transpose | solution.py:46
  1192.3 23.7 %reshape.231 = bf16[64,2,64,1024]{3,2,0,1:T(8,128)(2,1)} reshape(bf16[64,2,8,4,2048]{4,3,2,0,1:T(4,128)(2,1)} %copy.36) | data formatting | bytes 33554432 | tf_op jit(solution)/shard_map/reshape | solution.py:46
  1216.1 26.7 %fusion.1 = f32[2,1024,64,64]{1,3,2,0:T(8,128)} fusion(bf16[64,2,64,1024]{3,2,0,1:T(8,128)(2,1)} %reshape.231, bf16[2,1024,2,1024]{3,1,0,2:T(8,128)(2,1)} %copy_multiply_fusion), kind=kOutput, calls=%fused_computation.7 | convolution fusion | flops 17179869184 | bytes 54525952 | tf_op jit(solution)/shard_map/hrk,ahsk->hras/dot_general | solution.py:47
  1242.8 32.1 %multiply_reduce_fusion = (f32[2,1024]{1,0:T(2,128)S(1)}, bf16[2,1024,64,64]{1,3,2,0:T(8,128)(2,1)}) fusion(f32[2,1024]{1,0:T(2,128)S(1)} %bitcast.67, f32[2,64,64]{2,1,0:T(8,128)S(1)} %convolution_add_fusion.1, pred[2,64,64]{2,1,0:T(8,128)(4,1)S(1)} %iota_compare_fusion, pred[2,1024,64]{1,2,0:T(8,128)(4,1)S(1)} %broadcast_and_fusion, ...), kind=kOutput, calls=%fused_computation | convolution fusion | flops 17246976000 | bytes 71491584 | tf_op jit(solution)/shard_map/hrk,ahsk->hras/dot_general | solution.py:47
  1275.9 21.2 %copy.41 = bf16[2,1024,4096]{2,1,0:T(8,128)(2,1)} copy(bf16[2,1024,4096]{1,2,0:T(8,128)(2,1)} %bitcast.64) | data formatting | bytes 33554432
  1297.2 39.7 %reduce-scatter.4.cloned.1.call-done = f32[128,2]{1,0:T(8,128)} async-done(((f32[1024,2]{1,0:T(8,128)}), f32[128,2]{1,0:T(8,128)}) %reduce-scatter.4.cloned.1.call-update) | async-done | bytes 1040
  (44 shorter events, 37.3 us)
Async XLA Ops:
  7.2 22.1 %copy-start = (bf16[2,512,8,2048]{3,2,1,0:T(8,128)(2,1)S(1)}, bf16[2,512,8,2048]{3,2,1,0:T(8,128)(2,1)}, u32[]{:S(2)}) copy-start(bf16[2,512,8,2048]{3,2,1,0:T(8,128)(2,1)} %param.8) | copy-start | bytes 100663296
  411.4 368.3 %all-to-all-start = ((bf16[8,64,8,2048]{3,2,1,0:T(8,128)(2,1)}), bf16[8,64,8,2048]{3,2,1,0:T(8,128)(2,1)}, u32[]{:S(2)}, u32[]{:S(2)}) async-start(bf16[8,64,8,2048]{3,2,1,0:T(8,128)(2,1)} %get-tuple-element.15), calls=%async_computation | async-start | bytes 33554432 | tf_op jit(solution)/shard_map/all_to_all | solution.py:12
  779.7 190.0 %all-to-all-start.3 = ((bf16[64,8,16384]{2,0,1:T(8,128)(2,1)}), bf16[64,8,16384]{2,0,1:T(8,128)(2,1)}, u32[]{:S(2)}, u32[]{:S(2)}) async-start(bf16[64,8,16384]{2,0,1:T(8,128)(2,1)} %reshape.242), calls=%async_computation.3 | async-start | bytes 33554432 | tf_op jit(solution)/shard_map/all_to_all | solution.py:42
  830.9 146.1 %copy-start.2 = (f32[512]{0:T(512)S(1)}, f32[512]{0:T(512)}, u32[]{:S(2)}) copy-start(f32[512]{0:T(512)} %param.13) | copy-start | bytes 6148
  830.9 146.2 %copy-start.3 = (s32[8]{0:T(128)S(1)}, s32[8]{0:T(128)}, u32[]{:S(2)}) copy-start(s32[8]{0:T(128)} %param.9) | copy-start | bytes 100
  831.0 146.2 %copy-start.5 = (s32[8]{0:T(128)S(1)}, s32[8]{0:T(128)}, u32[]{:S(2)}) copy-start(s32[8]{0:T(128)} %param.10) | copy-start | bytes 100
  831.0 146.6 %copy-start.1 = (s32[2,1024,2]{1,2,0:T(2,128)S(1)}, s32[2,1024,2]{1,2,0:T(2,128)}, u32[]{:S(2)}) copy-start(s32[2,1024,2]{1,2,0:T(2,128)} %param.11) | copy-start | bytes 49156
  831.0 146.6 %copy-start.4 = (f32[100]{0:T(128)S(1)}, f32[100]{0:T(128)}, u32[]{:S(2)}) copy-start(f32[100]{0:T(128)} %param.12) | copy-start | bytes 1204
  969.7 190.1 %all-to-all-start.1 = ((bf16[64,8,16384]{2,0,1:T(8,128)(2,1)}), bf16[64,8,16384]{2,0,1:T(8,128)(2,1)}, u32[]{:S(2)}, u32[]{:S(2)}) async-start(bf16[64,8,16384]{2,0,1:T(8,128)(2,1)} %reshape.241), calls=%async_computation.1 | async-start | bytes 33554432 | tf_op jit(solution)/shard_map/all_to_all | solution.py:42
  976.8 360.1 %reduce-scatter.4.cloned.1.call-start = ((), (), s32[]{:S(2)}) async-start(), calls=%async_computation.5 | async-start | bytes 589824
Sparse Core Ops, SparseCore 0:
  1276.0 60.7 reduce-scatter.3
